TPU v7x, 512 devices: a whole 4x4x16 slice. The times are simulated.
512 devices in a mesh: dp: 8 (over x_hi, y), fsdp: 64 (over z, x_lo, core).
Axes of the slice: x: 4 (x_hi: 2, x_lo: 2; x = x_hi * 2 + x_lo), y: 4, z: 16, core: 2. Of those that a mesh axis runs over, the one named last changes fastest.
Arguments:
- samples: bfloat16 [1024, 256, 768], P(('dp', 'fsdp')), may hold values from -6 to 6
- cotangent: bfloat16 [1024, 256, 768], P(('dp', 'fsdp')), may hold values from -6 to 6
- w_in: bfloat16 [3072, 768], P('fsdp'), may hold values from -0.21875 to 0.21875
- w_out: bfloat16 [3072, 768], P('fsdp'), may hold values from -0.21875 to 0.21875
- sketch_in: bfloat16 [768, 16], replicated, may hold values from -0.21875 to 0.21875
- sketch_hidden: bfloat16 [3072, 16], replicated, may hold values from -0.109375 to 0.109375
- targets: float32 [1024], P(('dp', 'fsdp')), may hold values from -6 to 6
Outputs:
- coeffs: float32 [1024], P(('dp', 'fsdp'))
- sketched_step: float32 [512], replicated
All inputs are finite; a program needn't handle non-finite values.
Results may differ from a plain program's by a relative error of at most 0.0054.
Values may be sent and summed in bfloat16 or wider, within the bound.
A program may use at most 64 MiB of HBM per device.

v0:
```python
import jax
import jax.numpy as jnp
from jax import lax
from jax.experimental import pallas as pl
from jax.experimental.pallas import tpu as pltpu
from jax.sharding import PartitionSpec as P

DAMPING = 0.5
NZ, NY, NX = 16, 4, 4
MESH = pl.DeviceIdType.MESH


def position():
    group, member = lax.axis_index("dp"), lax.axis_index("fsdp")
    x = (group // 4) * 2 + (member // 2) % 2
    return x, group % 4, member // 4, member % 2


def device(x, y, z, core):
    return ((x // 2) * 4 + y, z * 4 + (x % 2) * 2 + core)


def greet(partners):
    barrier = pltpu.get_barrier_semaphore()
    for partner in partners:
        pl.semaphore_signal(barrier, inc=1, device_id=partner, device_id_type=MESH)
    pl.semaphore_wait(barrier, len(partners))


def weights_kernel(
    x_ref, g_ref, w_ref, all_ref, px_ref, pg_ref,
    swap_send, swap_recv, local_sem, z_send, z_recv, y_send, y_recv, o_send, o_recv, x_send, x_recv,
):
    x, y, z, core = position()
    low = x % 2
    up, down = (z + 1) % NZ, (z + NZ - 1) % NZ
    y_up, y_down = (y + 1) % NY, (y + NY - 1) % NY
    x_up, x_down = (x + 1) % NX, (x + NX - 1) % NX
    greet([
        device(x, y, up, core), device(x, y, down, core),
        device(x, y_up, z, core), device(x, y_down, z, core),
        device(x_up, y, z, core), device(x_down, y, z, core),
        device(x, y, z, 1 - core),
    ])
    sends = []

    def place(zz, q, lo):
        return all_ref.at[q // 2, zz, lo, q % 2]

    def remote(src, dst, send, recv, target):
        return pltpu.make_async_remote_copy(
            src_ref=src, dst_ref=dst, send_sem=send, recv_sem=recv, device_id=target, device_id_type=MESH
        )

    def start(copy):
        copy.start()
        sends.append(copy)

    def send_x(src, zz, q):
        target = device((x + (q // 2) * 2 + NX - 1) % NX, y, z, core)
        start(remote(src, place(zz, q, low), x_send.at[zz, q], x_recv.at[zz, q], target))

    def send_y(src, zz):
        start(remote(src, place(zz, y, low), y_send.at[0, zz], y_recv.at[0, zz], device(x, y_up, z, core)))
        start(remote(src, place(zz, y, low), y_send.at[1, zz], y_recv.at[1, zz], device(x, y_down, z, core)))

    def wait_recv(dst, recv):
        remote(dst, dst, swap_send.at[0], recv, device(x, y, z, 1 - core)).wait_recv()

    mine = w_ref.at[y // 2, y % 2]
    start(remote(mine, place(z, y, low), z_send.at[0, 1], z_recv.at[0, 1], device(x, y, up, core)))
    start(remote(mine, place(z, y, low), z_send.at[1, 1], z_recv.at[1, 1], device(x, y, down, core)))
    for q in range(4):
        send_x(w_ref.at[q // 2, q % 2], z, q)
    locals_ = []
    for q in range(4):
        copy = pltpu.make_async_copy(w_ref.at[q // 2, q % 2], place(z, q, low), local_sem.at[q])
        copy.start()
        locals_.append(copy)
    start(remote(x_ref, px_ref, swap_send.at[0], swap_recv.at[0], device(x, y, z, 1 - core)))
    start(remote(g_ref, pg_ref, swap_send.at[1], swap_recv.at[1], device(x, y, z, 1 - core)))

    def blocks_of(step):
        found = []
        if 1 <= step <= 8:
            found.append((0, (z + NZ - step) % NZ))
        if 1 <= step <= 7:
            found.append((1, (z + step) % NZ))
        return found

    for step in range(1, 11):
        for way, zz in blocks_of(step):
            here = place(zz, y, low)
            wait_recv(here, z_recv.at[way, step])
            if step < (8 if way == 0 else 7):
                target = device(x, y, up if way == 0 else down, core)
                start(remote(here, here, z_send.at[way, step + 1], z_recv.at[way, step + 1], target))
            send_y(here, zz)
            send_x(here, zz, y)
        for way, zz in blocks_of(step - 1):
            below, above = place(zz, y_down, low), place(zz, y_up, low)
            wait_recv(below, y_recv.at[0, zz])
            wait_recv(above, y_recv.at[1, zz])
            if way == 0:
                start(remote(below, below, o_send.at[zz], o_recv.at[zz], device(x, y_up, z, core)))
            else:
                start(remote(above, above, o_send.at[zz], o_recv.at[zz], device(x, y_down, z, core)))
            send_x(below, zz, y_down)
            send_x(above, zz, y_up)
        for way, zz in blocks_of(step - 2):
            far = (y + 2) % NY
            wait_recv(place(zz, far, low), o_recv.at[zz])
            send_x(place(zz, far, low), zz, far)
    for zz in range(NZ):
        for q in range(4):
            wait_recv(place(zz, q, 1 - low), x_recv.at[zz, q])
    wait_recv(px_ref, swap_recv.at[0])
    wait_recv(pg_ref, swap_recv.at[1])
    for copy in locals_:
        copy.wait()
    for copy in sends:
        copy.wait_send()


def gather_weights(flat_x, flat_g, w_in, w_out):
    rows, width = w_in.shape
    half = rows // 2
    w = jnp.stack([w_in, w_out]).reshape(2, 2, half, width)
    anywhere = pl.BlockSpec(memory_space=pl.ANY)
    sem = pltpu.SemaphoreType.DMA
    return pl.pallas_call(
        weights_kernel,
        out_shape=(
            jax.ShapeDtypeStruct((2, NZ, 2, 2, half, width), w.dtype),
            jax.ShapeDtypeStruct(flat_x.shape, flat_x.dtype),
            jax.ShapeDtypeStruct(flat_g.shape, flat_g.dtype),
        ),
        in_specs=[anywhere] * 3,
        out_specs=(anywhere,) * 3,
        scratch_shapes=[
            sem((2,)), sem((2,)), sem((4,)), sem((2, 9)), sem((2, 9)), sem((2, NZ)), sem((2, NZ)),
            sem((NZ,)), sem((NZ,)), sem((NZ, 4)), sem((NZ, 4)),
        ],
        compiler_params=pltpu.CompilerParams(collective_id=0, has_side_effects=True),
        name="gather_weights",
    )(flat_x, flat_g, w)


def features_kernel(
    own_ref, other_ref, targets_ref, f_ref, got, zbuf, wide,
    swap_send, swap_recv, a_send, a_recv, b_send, b_recv, y_send, y_recv, x_send, x_recv, c_send, c_recv,
):
    x, y, z, core = position()
    high, low = z // 4, z % 4
    near = [device(x, y, high * 4 + (low + d) % 4, core) for d in range(1, 4)]
    far = [device(x, y, ((high + d) % 4) * 4 + low, core) for d in range(1, 4)]
    along_y = [device(x, (y + d) % NY, z, core) for d in range(1, 4)]
    along_x = [device((x + d) % NX, y, z, core) for d in range(1, 4)]
    partner = device(x, y, z, 1 - core)
    greet(near + far + along_y + along_x + [partner])

    def remote(src, dst, send, recv, target):
        return pltpu.make_async_remote_copy(
            src_ref=src, dst_ref=dst, send_sem=send, recv_sem=recv, device_id=target, device_id_type=MESH
        )

    def exchange(mine, theirs, send, recv, partners):
        copies = []
        for d, target in enumerate(partners):
            copy = remote(mine, mine, send.at[d], recv.at[d], target)
            copy.start()
            copies.append(copy)
        for d in range(len(partners)):
            remote(theirs[d], theirs[d], send.at[d], recv.at[d], partners[d]).wait_recv()
        return copies

    swap = remote(other_ref, got, swap_send, swap_recv, partner)
    swap.start()
    swap.wait_recv()
    feats = own_ref[...] + got[...]
    t = targets_ref[...]
    high_t = t.astype(jnp.bfloat16).astype(jnp.float32)
    mid_t = (t - high_t).astype(jnp.bfloat16).astype(jnp.float32)
    low_t = t - high_t - mid_t
    lane = lax.broadcasted_iota(jnp.int32, (2, 128), 1)
    tail = jnp.where(lane == 0, high_t, jnp.where(lane == 1, mid_t, jnp.where(lane == 2, low_t, 0.0)))
    size = feats.shape[1]
    zbuf[z, :, 0:size] = feats.astype(jnp.bfloat16)
    zbuf[z, :, size:] = tail.astype(jnp.bfloat16)
    sends = [swap]
    sends += exchange(
        zbuf.at[z], [zbuf.at[high * 4 + (low + 4 - d) % 4] for d in range(1, 4)], a_send, a_recv, near
    )
    sends += exchange(
        zbuf.at[pl.ds(high * 4, 4)],
        [zbuf.at[pl.ds(((high + 4 - d) % 4) * 4, 4)] for d in range(1, 4)],
        b_send, b_recv, far,
    )
    for zz in range(NZ):
        wide[2 * zz:2 * zz + 2, :] = zbuf[zz].astype(jnp.float32)
    base = core * 16 + x * 4
    f_ref[base + y] = wide[...].astype(jnp.bfloat16)
    sends += exchange(
        f_ref.at[base + y], [f_ref.at[base + (y + 4 - d) % NY] for d in range(1, 4)], y_send, y_recv, along_y
    )
    sends += exchange(
        f_ref.at[pl.ds(base, 4)],
        [f_ref.at[pl.ds(core * 16 + ((x + 4 - d) % NX) * 4, 4)] for d in range(1, 4)],
        x_send, x_recv, along_x,
    )
    sends += exchange(
        f_ref.at[pl.ds(core * 16, 16)], [f_ref.at[pl.ds((1 - core) * 16, 16)]], c_send, c_recv, [partner]
    )
    for copy in sends:
        copy.wait_send()


def gather_features(own, other, targets):
    size = own.shape[1]
    inside = pl.BlockSpec(memory_space=pltpu.VMEM)
    sem = pltpu.SemaphoreType.DMA
    return pl.pallas_call(
        features_kernel,
        out_shape=jax.ShapeDtypeStruct((32, 32, size + 128), jnp.bfloat16),
        in_specs=[inside] * 3,
        out_specs=inside,
        scratch_shapes=[
            pltpu.VMEM((2, size), jnp.float32),
            pltpu.VMEM((NZ, 2, size + 128), jnp.bfloat16),
            pltpu.VMEM((32, size + 128), jnp.float32),
            sem, sem, sem((3,)), sem((3,)), sem((3,)), sem((3,)), sem((3,)), sem((3,)),
            sem((3,)), sem((3,)), sem((1,)), sem((1,)),
        ],
        compiler_params=pltpu.CompilerParams(collective_id=1, has_side_effects=True),
        name="gather_features",
    )(own, other, targets)


def invert(m):
    side = m.shape[0]
    lane = lax.broadcasted_iota(jnp.int32, m.shape, 1)
    sub = lax.broadcasted_iota(jnp.int32, m.shape, 0)
    for k in range(0, side, 2):
        j = k + 1
        c0 = jnp.broadcast_to(m[:, k:k + 1], m.shape)
        c1 = jnp.broadcast_to(m[:, j:j + 1], m.shape)
        inv0 = 1.0 / c0[k:k + 1, :]
        r0 = jnp.where(lane[0:1] == k, 1.0, m[k:k + 1, :]) * inv0
        r1 = jnp.where(lane[0:1] == k, 0.0, m[j:j + 1, :]) - c0[j:j + 1, :] * r0
        across = c1[k:k + 1, :] * inv0
        inv1 = 1.0 / (c1[j:j + 1, :] - c0[j:j + 1, :] * across)
        r1 = jnp.where(lane[0:1] == j, 1.0, r1) * inv1
        c0 = jnp.where(sub == k, -1.0, c0)
        c1 = jnp.where(sub == k, 0.0, c1) - c0 * across
        c1 = jnp.where(sub == j, -1.0, c1)
        m = jnp.where((lane == k) | (sub == k), 0.0, m) - c0 * r0
        m = jnp.where((lane == j) | (sub == j), 0.0, m) - c1 * r1
    return m


def solve_kernel(a_ref, out_ref, work):
    size = a_ref.shape[0]
    side = 128
    high = lax.Precision.HIGHEST
    diagonal = lax.broadcasted_iota(jnp.int32, a_ref.shape, 0) == lax.broadcasted_iota(jnp.int32, a_ref.shape, 1)
    work[...] = a_ref[...] + jnp.where(diagonal, DAMPING, 0.0)

    def body(block, carry):
        here = pl.ds(pl.multiple_of(block * side, side), side)
        rows = jnp.dot(invert(work[here, here]), work[here, :], precision=high, preferred_element_type=jnp.float32)
        work[...] = work[...] - jnp.dot(work[:, here], rows, precision=high, preferred_element_type=jnp.float32)
        work[here, :] = rows
        return carry

    lax.fori_loop(0, size // side, body, 0)
    out_ref[...] = lax.dot_general(
        jnp.ones((8, a_ref.shape[1] - size), jnp.float32),
        work[:, size:],
        (((1,), (1,)), ((), ())),
        precision=high,
        preferred_element_type=jnp.float32,
    )


def solve(extended):
    return pl.pallas_call(
        solve_kernel,
        out_shape=jax.ShapeDtypeStruct((8, extended.shape[0]), jnp.float32),
        in_specs=[pl.BlockSpec(memory_space=pltpu.VMEM)],
        out_specs=pl.BlockSpec(memory_space=pltpu.VMEM),
        scratch_shapes=[pltpu.VMEM(extended.shape, jnp.float32)],
        name="solve",
    )(extended)[0]


def partial_features(flat_x, flat_g, rows_in, rows_out, sketch_in, sketch_rows, count):
    pre = lax.dot_general(flat_x, rows_in, (((1,), (1,)), ((), ())), preferred_element_type=jnp.float32)
    back = lax.dot_general(flat_g, rows_out, (((1,), (1,)), ((), ())), preferred_element_type=jnp.float32)
    sig = jax.nn.sigmoid(pre)
    hidden = (pre * sig).astype(jnp.bfloat16)
    slope = (back * sig * (1.0 + pre * (1.0 - sig))).astype(jnp.bfloat16)
    hq = jnp.dot(hidden, sketch_rows, preferred_element_type=jnp.float32)
    dq = jnp.dot(slope, sketch_rows, preferred_element_type=jnp.float32)
    xp = jnp.dot(flat_x, sketch_in, preferred_element_type=jnp.float32)
    gp = jnp.dot(flat_g, sketch_in, preferred_element_type=jnp.float32)
    length = flat_x.shape[0] // count

    def outer(left, right):
        return (
            jnp.einsum(
                "spr,spq->srq",
                left.reshape(count, length, -1),
                right.reshape(count, length, -1),
                precision=lax.Precision.HIGHEST,
            )
            / length
        ).reshape(count, -1)

    return jnp.concatenate([outer(dq, xp), outer(hq, gp)], axis=1)


def per_device(samples, cotangent, w_in, w_out, sketch_in, sketch_hidden, targets):
    count, length, width = samples.shape
    flat_x = samples.reshape(count * length, width)
    flat_g = cotangent.reshape(count * length, width)
    rows = w_in.shape[0]
    weights, other_x, other_g = gather_weights(flat_x, flat_g, w_in, w_out)
    rows_in, rows_out = weights[0].reshape(-1, width), weights[1].reshape(-1, width)
    core = lax.axis_index("fsdp") % 2
    sketch_rows = lax.dynamic_index_in_dim(
        sketch_hidden.reshape(NZ * 2, 2, rows, -1), core, 1, keepdims=False
    ).reshape(NZ * 2 * rows, -1)
    own = partial_features(flat_x, flat_g, rows_in, rows_out, sketch_in, sketch_rows, count)
    other = partial_features(other_x, other_g, rows_in, rows_out, sketch_in, sketch_rows, count)
    table = gather_features(own, other, targets.reshape(count, 1))
    size = own.shape[1]
    table = table.reshape(-1, size + 128)
    everyone = table[:, :size]
    extended = lax.dot_general(
        everyone, table, (((0,), (0,)), ((), ())), preferred_element_type=jnp.float32
    )
    step = solve(extended)
    x, y, z, core = position()
    start = (core * 16 + x * 4 + y) * 32 + z * count
    feats = lax.dynamic_slice_in_dim(everyone, start, count, 0)
    fitted = jnp.dot(feats.astype(jnp.float32), step, precision=lax.Precision.HIGHEST)
    coeffs = (targets - fitted) / DAMPING
    return (coeffs, step)


def solution(mesh):
    in_specs = (
        P(("dp", "fsdp"), None, None),
        P(("dp", "fsdp"), None, None),
        P("fsdp", None),
        P("fsdp", None),
        P(),
        P(),
        P(("dp", "fsdp")),
    )
    out_specs = (P(("dp", "fsdp")), P())
    return jax.shard_map(
        per_device, mesh=mesh, in_specs=in_specs, out_specs=out_specs, check_vma=False
    )
```

profile of v0, /device:TPU:1, one launch (start us, length us, event | category | flops | bytes accessed | tf_op | source)
XLA Modules:
  0.0 165.7 jit_solution(8865329919915716653)
XLA Ops:
  0.6 0.0 copy-start
  0.7 1.3 copy.15.targets_ref
  2.0 0.0 copy-done
  2.0 1.4 fusion.13
  3.5 1.5 fusion.11
  4.9 1.6 pad_maximum_fusion.w_ref
  6.5 1.2 reshape.62
  7.7 0.9 dynamic-slice_reduce_fusion
  8.6 0.2 reshape.72
  8.7 49.1 %gather_weights.1 = (bf16[2,16,2,2,24,768]{5,4,3,2,1,0:T(8,128)(2,1)}, bf16[512,768]{1,0:T(8,128)(2,1)}, bf16[512,768]{1,0:T(8,128)(2,1)}) custom-call(bf16[512,768]{1,0:T(8,128)(2,1)} %bitcast.80, bf16[512,768]{1,0:T(8,128)(2,1)} %bitcast.82, bf16[2,2,24,768]{3,2,1,0:T(8,128)(2,1)} %pad_maximum_fusion.w_ref), custom_call_target="tpu_custom_call" | custom-call | tf_op jit(solution)/shard_map/gather_weights/pallas_call | solution.py:131
  57.9 0.0 copy-start.4
  57.9 0.0 copy-start.5
  57.9 2.9 %fusion.21 = (bf16[1,16,2,2,24,768]{5,4,3,2,1,0:T(8,128)(2,1)S(1)}, bf16[1,16,2,2,24,768]{5,4,3,2,1,0:T(8,128)(2,1)S(1)}) fusion(bf16[2,16,2,2,24,768]{5,4,3,2,1,0:T(8,128)(2,1)} %get-tuple-element.5), kind=kLoop, calls=%fused_computation.37 | loop fusion | bytes 9437184 | tf_op jit(solution)/shard_map/slice | solution.py:328
  60.7 0.0 copy-start.3
  60.7 0.0 copy-done.4
  60.8 0.3 fusion.27
  61.1 0.0 copy-done.5
  61.1 0.3 fusion.25
  61.4 3.3 %multiply_convert_fusion = (bf16[512,1536]{1,0:T(8,128)(2,1)S(1)}, f32[512,1536]{1,0:T(8,128)}) fusion(bf16[512,768]{1,0:T(8,128)(2,1)S(1)} %copy-done.5, bf16[1536,768]{1,0:T(8,128)(2,1)S(1)} %bitcast.86), kind=kOutput, calls=%fused_computation.6 | convolution fusion | flops 1211891712 | bytes 7864320 | tf_op jit(solution)/shard_map/dot_general | solution.py:297
  64.7 0.0 copy-done.3
  64.7 0.5 fusion.26
  65.2 0.2 convolution_multiply_fusion.1
  65.4 0.1 reshape.69
  65.5 0.0 copy-start.1
  65.5 4.1 %fusion.4 = bf16[512,1536]{1,0:T(8,128)(2,1)S(1)} fusion(f32[512,1536]{1,0:T(8,128)} %get-tuple-element.13, bf16[512,768]{1,0:T(8,128)(2,1)} %get-tuple-element.6, bf16[1536,768]{1,0:T(8,128)(2,1)S(1)} %bitcast.84), kind=kOutput, calls=%fused_computation.11 | convolution fusion | flops 1215037440 | bytes 7864320 | tf_op jit(solution)/shard_map/dot_general | solution.py:298
  69.6 0.5 fusion.24
  70.1 0.2 convolution_multiply_fusion.2
  70.3 0.1 reshape.67
  70.4 0.0 copy-done.1
  70.4 0.0 copy-start.2
  70.4 3.5 %multiply_convert_fusion.1 = (bf16[512,1536]{1,0:T(8,128)(2,1)S(1)}, f32[512,1536]{1,0:T(8,128)S(1)}) fusion(bf16[1536,768]{1,0:T(8,128)(2,1)} %bitcast.87, bf16[512,768]{1,0:T(8,128)(2,1)S(1)} %bitcast.81), kind=kOutput, calls=%fused_computation.8 | convolution fusion | flops 1211891712 | bytes 7864320 | tf_op jit(solution)/shard_map/dot_general | solution.py:297
  73.9 0.0 copy-done.2
  73.9 3.1 %fusion.3 = bf16[512,1536]{1,0:T(8,128)(2,1)} fusion(f32[512,1536]{1,0:T(8,128)S(1)} %get-tuple-element.11, bf16[1536,768]{1,0:T(8,128)(2,1)S(1)} %bitcast.85, bf16[512,768]{1,0:T(8,128)(2,1)S(1)} %bitcast.83), kind=kOutput, calls=%fused_computation.10 | convolution fusion | flops 1215037440 | bytes 7864320 | tf_op jit(solution)/shard_map/dot_general | solution.py:298
  77.0 0.5 fusion.23
  77.5 0.2 convolution_multiply_fusion.3
  77.7 0.1 reshape.65
  77.8 1.9 %fusion.22 = f32[2,256,16]{1,2,0:T(8,128)S(1)} fusion(bf16[2,256,1536]{2,1,0:T(8,128)(2,1)} %bitcast.88, bf16[1536,16,1]{0,1,2:T(8,128)(2,1)S(1)} %reshape.72), kind=kOutput, calls=%fused_computation.38 | convolution fusion | flops 25165824 | bytes 1654784 | tf_op jit(solution)/shard_map/dot_general | solution.py:303
  79.7 0.2 convolution_multiply_fusion.4
  79.9 0.1 reshape.64
  80.0 0.6 pad_maximum_fusion.1
  80.6 40.2 %gather_features.1 = bf16[32,32,640]{2,1,0:T(8,128)(2,1)} custom-call(f32[2,512]{1,0:T(2,128)} %get-tuple-element.14.own_ref, f32[2,512]{1,0:T(2,128)} %get-tuple-element.15.other_ref, f32[2,1]{1,0:T(2,128)} %copy.15.targets_ref), custom_call_target="tpu_custom_call" | custom-call | tf_op jit(solution)/shard_map/gather_features/pallas_call | solution.py:222
  120.8 1.3 slice.16
  122.1 0.0 copy-start.6
  122.1 3.9 %fusion.19.a_ref = f32[512,640]{1,0:T(8,128)} fusion(bf16[1024,640]{1,0:T(8,128)(2,1)} %bitcast.79), kind=kOutput, calls=%fused_computation.35 | convolution fusion | flops 671088640 | bytes 3670016 | tf_op jit(solution)/shard_map/dot_general | solution.py:339
  126.1 37.0 %solve.1 = f32[8,512]{1,0:T(8,128)} custom-call(f32[512,640]{1,0:T(8,128)} %fusion.19.a_ref), custom_call_target="tpu_custom_call" | custom-call | tf_op jit(solution)/shard_map/solve/pallas_call | solution.py:286
  163.0 0.0 copy-done.6
  163.0 1.4 fusion.6
  164.4 1.3 slice.17
Async XLA Ops:
  0.6 1.4 copy-start
  57.9 2.9 %copy-start.4 = (bf16[512,768]{1,0:T(8,128)(2,1)S(1)}, bf16[512,768]{1,0:T(8,128)(2,1)}, u32[]{:S(2)}) copy-start(bf16[512,768]{1,0:T(8,128)(2,1)} %get-tuple-element.6) | copy-start | bytes 2359300
  57.9 3.2 %copy-start.5 = (bf16[512,768]{1,0:T(8,128)(2,1)S(1)}, bf16[512,768]{1,0:T(8,128)(2,1)}, u32[]{:S(2)}) copy-start(bf16[512,768]{1,0:T(8,128)(2,1)} %get-tuple-element.7) | copy-start | bytes 2359300
  60.7 4.0 %copy-start.3 = (bf16[1,16,2,2,24,768]{5,4,3,2,1,0:T(8,128)(2,1)}, bf16[1,16,2,2,24,768]{5,4,3,2,1,0:T(8,128)(2,1)S(1)}, u32[]{:S(2)}) copy-start(bf16[1,16,2,2,24,768]{5,4,3,2,1,0:T(8,128)(2,1)S(1)} %get-tuple-element.9) | copy-start | bytes 7077892
  65.5 4.9 %copy-start.1 = (bf16[2,256,768]{2,1,0:T(8,128)(2,1)S(1)}, bf16[2,256,768]{2,1,0:T(8,128)(2,1)}, u32[]{:S(2)}) copy-start(bf16[2,256,768]{2,1,0:T(8,128)(2,1)} %param.7) | copy-start | bytes 2359300
  70.4 3.5 %copy-start.2 = (bf16[2,256,768]{2,1,0:T(8,128)(2,1)S(1)}, bf16[2,256,768]{2,1,0:T(8,128)(2,1)}, u32[]{:S(2)}) copy-start(bf16[2,256,768]{2,1,0:T(8,128)(2,1)} %param.8) | copy-start | bytes 2359300
  122.1 40.9 %copy-start.6 = (f32[2]{0:T(128)S(1)}, f32[2]{0:T(128)}, u32[]{:S(2)}) copy-start(f32[2]{0:T(128)} %param.13) | copy-start | bytes 28
where the time goes:
time: 166 us
  Pallas kernels  126 us (76%)
  matrix products  26.9 us (16%)
  local copies, waits for them, and re-layouts  9.4 us (6%)
  other arithmetic  2.22 us (1%)
    pallas_call x1, Pallas kernels, gather_weights(): pl.pallas_call(weights_kernel, out_shape=(jax.ShapeDtypeStruct((2, NZ, 2,...  49.1 us
    pallas_call x1, Pallas kernels, gather_features(): pl.pallas_call(features_kernel, out_shape=jax.ShapeDtypeStruct((32, 32, s...  40.2 us
    pallas_call x1, Pallas kernels, solve(): pl.pallas_call(solve_kernel, out_shape=jax.ShapeDtypeStruct((8, extended....  37 us
    dot_general x2, matrix products, partial_features(): lax.dot_general(flat_g, rows_out, (((1,), (1,)), ((), ())), preferred_ele...  7.22 us
    dot_general x2, matrix products, partial_features(): lax.dot_general(flat_x, rows_in, (((1,), (1,)), ((), ())), preferred_elem...  6.82 us
    dot_general x1, matrix products, per_device(): lax.dot_general(everyone, table, (((0,), (0,)), ((), ())), preferred_elem...  3.92 us

commit v1 on v0

--- a/solution.py
+++ b/solution.py
@@ -293,45 +293,77 @@
     )(extended)[0]
 
 
-def partial_features(flat_x, flat_g, rows_in, rows_out, sketch_in, sketch_rows, count):
-    pre = lax.dot_general(flat_x, rows_in, (((1,), (1,)), ((), ())), preferred_element_type=jnp.float32)
-    back = lax.dot_general(flat_g, rows_out, (((1,), (1,)), ((), ())), preferred_element_type=jnp.float32)
-    sig = jax.nn.sigmoid(pre)
-    hidden = (pre * sig).astype(jnp.bfloat16)
-    slope = (back * sig * (1.0 + pre * (1.0 - sig))).astype(jnp.bfloat16)
-    hq = jnp.dot(hidden, sketch_rows, preferred_element_type=jnp.float32)
-    dq = jnp.dot(slope, sketch_rows, preferred_element_type=jnp.float32)
-    xp = jnp.dot(flat_x, sketch_in, preferred_element_type=jnp.float32)
-    gp = jnp.dot(flat_g, sketch_in, preferred_element_type=jnp.float32)
-    length = flat_x.shape[0] // count
-
-    def outer(left, right):
-        return (
-            jnp.einsum(
-                "spr,spq->srq",
-                left.reshape(count, length, -1),
-                right.reshape(count, length, -1),
-                precision=lax.Precision.HIGHEST,
-            )
-            / length
-        ).reshape(count, -1)
-
-    return jnp.concatenate([outer(dq, xp), outer(hq, gp)], axis=1)
+def block_kernel(
+    x_ref, g_ref, other_x_ref, other_g_ref, w_ref, sketch_ref, sketch_in_ref, out_ref, hq_ref, dq_ref
+):
+    step = pl.program_id(0)
+    length = x_ref.shape[1]
+
+    @pl.when(step == 0)
+    def _():
+        hq_ref[...] = jnp.zeros_like(hq_ref)
+        dq_ref[...] = jnp.zeros_like(dq_ref)
+
+    pairs = [(x_ref, g_ref, 0), (x_ref, g_ref, 1), (other_x_ref, other_g_ref, 0), (other_x_ref, other_g_ref, 1)]
+    sketch = sketch_ref[...]
+    across = (((1,), (1,)), ((), ()))
+    for n, (xs, gs, at) in enumerate(pairs):
+        pre = lax.dot_general(xs[at], w_ref[0], across, preferred_element_type=jnp.float32)
+        back = lax.dot_general(gs[at], w_ref[1], across, preferred_element_type=jnp.float32)
+        sig = jax.nn.sigmoid(pre)
+        hidden = (pre * sig).astype(jnp.bfloat16)
+        slope = (back * sig * (1.0 + pre * (1.0 - sig))).astype(jnp.bfloat16)
+        hq_ref[n] += jnp.dot(hidden, sketch, preferred_element_type=jnp.float32)
+        dq_ref[n] += jnp.dot(slope, sketch, preferred_element_type=jnp.float32)
+
+    @pl.when(step == pl.num_programs(0) - 1)
+    def _():
+        for n, (xs, gs, at) in enumerate(pairs):
+            xp = jnp.dot(xs[at], sketch_in_ref[...], preferred_element_type=jnp.float32)
+            gp = jnp.dot(gs[at], sketch_in_ref[...], preferred_element_type=jnp.float32)
+            for which, (left, right) in enumerate([(dq_ref[n], xp), (hq_ref[n], gp)]):
+                out_ref[n, which] = lax.dot_general(
+                    left, right, (((0,), (0,)), ((), ())),
+                    precision=lax.Precision.HIGHEST, preferred_element_type=jnp.float32,
+                ) * (1.0 / length)
+
+
+def partial_features(samples, cotangent, other_x, other_g, weights, sketch_rows, sketch_in):
+    count, length, width = samples.shape
+    hidden_units, rank = sketch_rows.shape
+    chunk = 256
+    whole = pl.BlockSpec((count, length, width), lambda i: (0, 0, 0))
+    return pl.pallas_call(
+        block_kernel,
+        grid=(hidden_units // chunk,),
+        out_shape=jax.ShapeDtypeStruct((2 * count, 2, rank, rank), jnp.float32),
+        in_specs=[whole] * 4 + [
+            pl.BlockSpec((2, chunk, width), lambda i: (0, i, 0)),
+            pl.BlockSpec((chunk, rank), lambda i: (i, 0)),
+            pl.BlockSpec((width, rank), lambda i: (0, 0)),
+        ],
+        out_specs=pl.BlockSpec((2 * count, 2, rank, rank), lambda i: (0, 0, 0, 0)),
+        scratch_shapes=[
+            pltpu.VMEM((2 * count, length, rank), jnp.float32),
+            pltpu.VMEM((2 * count, length, rank), jnp.float32),
+        ],
+        compiler_params=pltpu.CompilerParams(vmem_limit_bytes=48 * 2**20),
+        name="pointwise_block",
+    )(samples, cotangent, other_x, other_g, weights, sketch_rows, sketch_in)
 
 
 def per_device(samples, cotangent, w_in, w_out, sketch_in, sketch_hidden, targets):
     count, length, width = samples.shape
-    flat_x = samples.reshape(count * length, width)
-    flat_g = cotangent.reshape(count * length, width)
     rows = w_in.shape[0]
-    weights, other_x, other_g = gather_weights(flat_x, flat_g, w_in, w_out)
-    rows_in, rows_out = weights[0].reshape(-1, width), weights[1].reshape(-1, width)
+    weights, other_x, other_g = gather_weights(samples, cotangent, w_in, w_out)
     core = lax.axis_index("fsdp") % 2
     sketch_rows = lax.dynamic_index_in_dim(
         sketch_hidden.reshape(NZ * 2, 2, rows, -1), core, 1, keepdims=False
     ).reshape(NZ * 2 * rows, -1)
-    own = partial_features(flat_x, flat_g, rows_in, rows_out, sketch_in, sketch_rows, count)
-    other = partial_features(other_x, other_g, rows_in, rows_out, sketch_in, sketch_rows, count)
+    partial = partial_features(
+        samples, cotangent, other_x, other_g, weights.reshape(2, -1, width), sketch_rows, sketch_in
+    ).reshape(2 * count, -1)
+    own, other = partial[:count], partial[count:]
     table = gather_features(own, other, targets.reshape(count, 1))
     size = own.shape[1]
     table = table.reshape(-1, size + 128)

time: 166 us -> 153 us (0.922)
  matrix products: 26.9 us -> 4.36 us
  Pallas kernels: 126 us -> 139 us
  local copies, waits for them, and re-layouts: 9.4 us -> 7.45 us
    dot_general x16 -> x0, matrix products: 21.6 us -> none  [the longest x2 7.22 us: partial_features(): lax.dot_general(flat_g, rows_out, (((1,), (1,)), ((), ())), preferred_ele...]
    pallas_call x0 -> x1, Pallas kernels: none -> 13 us  [partial_features(): pl.pallas_call(block_kernel, grid=(hidden_units // chunk,), out_shape=jax...]
    unnamed x14 -> x22, local copies, waits for them, and re-layouts: 0.04 us -> 3.28 us
where the time goes in v1:
time: 153 us
  Pallas kernels  139 us (91%)
  local copies, waits for them, and re-layouts  7.45 us (5%)
  matrix products  4.36 us (3%)
    pallas_call x1, Pallas kernels, gather_weights(): pl.pallas_call(weights_kernel, out_shape=(jax.ShapeDtypeStruct((2, NZ, 2,...  49.1 us
    pallas_call x1, Pallas kernels, gather_features(): pl.pallas_call(features_kernel, out_shape=jax.ShapeDtypeStruct((32, 32, s...  40.2 us
    pallas_call x1, Pallas kernels, solve(): pl.pallas_call(solve_kernel, out_shape=jax.ShapeDtypeStruct((8, extended....  37 us
    pallas_call x1, Pallas kernels, partial_features(): pl.pallas_call(block_kernel, grid=(hidden_units // chunk,), out_shape=jax...  13 us
    dot_general x1, matrix products, per_device(): lax.dot_general(everyone, table, (((0,), (0,)), ((), ())), preferred_elem...  3.71 us
    unnamed x22, local copies, waits for them, and re-layouts  3.28 us

profile of v1, /device:TPU:1, one launch (start us, length us, event | category | flops | bytes accessed | tf_op | source)
XLA Modules:
  0.0 152.7 jit_solution(1549412986916282240)
XLA Ops:
  0.6 0.0 copy-start.7
  0.6 0.0 copy-start.6
  0.7 1.2 reshape.29
  1.9 0.3 constant_dynamic-slice_fusion
  2.2 0.0 copy-start.8
  2.2 0.0 copy-start
  2.2 0.0 copy-start.1
  2.2 0.3 copy.12
  2.5 0.0 copy-done.7
  2.5 0.0 copy-done.6
  2.5 0.7 pad_maximum_fusion.w_ref
  3.2 49.1 %gather_weights.1 = (bf16[2,16,2,2,24,768]{5,4,3,2,1,0:T(8,128)(2,1)}, bf16[2,256,768]{2,1,0:T(8,128)(2,1)}, bf16[2,256,768]{2,1,0:T(8,128)(2,1)}) custom-call(bf16[2,256,768]{2,1,0:T(8,128)(2,1)} %x_ref.3, bf16[2,256,768]{2,1,0:T(8,128)(2,1)} %g_ref.3, bf16[2,2,24,768]{3,2,1,0:T(8,128)(2,1)} %pad_maximum_fusion.w_ref), custom_call_target="tpu_custom_call" | custom-call | tf_op jit(solution)/shard_map/gather_weights/pallas_call | solution.py:131
  52.3 0.0 copy-done.8
  52.3 0.2 copy.10.sketch_in_ref
  52.5 0.0 copy-done
  52.5 0.0 copy-done.1
  52.5 0.0 copy-start.2
  52.5 1.1 copy-done.2
  53.6 0.0 copy-start.3
  53.6 1.1 copy-done.3
  54.7 0.0 copy-start.9
  54.7 13.0 %pointwise_block.1 = f32[4,2,16,16]{3,2,1,0:T(8,128)S(1)} custom-call(bf16[2,256,768]{2,1,0:T(8,128)(2,1)S(1)} %copy-done, bf16[2,256,768]{2,1,0:T(8,128)(2,1)S(1)} %copy-done.1, bf16[2,256,768]{2,1,0:T(8,128)(2,1)S(1)} %copy-done.2, bf16[2,256,768]{2,1,0:T(8,128)(2,1)S(1)} %copy-done.3, bf16[2,1536,768]{2,1,0:T(8,128)(2,1)} %bitcast.24, ...), custom_call_target="tpu_custom_call" | custom-call | tf_op jit(solution)/shard_map/pointwise_block/pallas_call | solution.py:336
  67.8 0.7 slice.19.own_ref
  68.5 0.7 slice.21.other_ref
  69.1 0.0 copy-done.9
  69.1 0.6 copy.11.targets_ref
  69.8 40.2 %gather_features.1 = bf16[32,32,640]{2,1,0:T(8,128)(2,1)} custom-call(f32[2,512]{1,0:T(2,128)} %slice.19.own_ref, f32[2,512]{1,0:T(2,128)} %slice.21.other_ref, f32[2,1]{1,0:T(2,128)} %copy.11.targets_ref), custom_call_target="tpu_custom_call" | custom-call | tf_op jit(solution)/shard_map/gather_features/pallas_call | solution.py:222
  110.0 3.7 %fusion.6.a_ref = f32[512,640]{1,0:T(8,128)} fusion(bf16[1024,640]{1,0:T(8,128)(2,1)} %bitcast.25), kind=kOutput, calls=%fused_computation.9 | convolution fusion | flops 671088640 | bytes 3670016 | tf_op jit(solution)/shard_map/dot_general | solution.py:371
  113.7 0.0 copy-start.4
  113.7 37.0 %solve.1 = f32[8,512]{1,0:T(8,128)} custom-call(f32[512,640]{1,0:T(8,128)} %fusion.6.a_ref), custom_call_target="tpu_custom_call" | custom-call | tf_op jit(solution)/shard_map/solve/pallas_call | solution.py:286
  150.8 0.0 copy-done.4
  150.8 0.0 copy-start.5
  150.8 0.1 slice.26
  150.9 0.6 copy-done.5
  151.5 0.6 fusion.1
  152.2 0.6 slice.27
  (1 shorter events, 0.0 us)
Async XLA Ops:
  0.6 1.9 %copy-start.7 = (bf16[48,768]{1,0:T(8,128)(2,1)S(1)}, bf16[48,768]{1,0:T(8,128)(2,1)}, u32[]{:S(2)}) copy-start(bf16[48,768]{1,0:T(8,128)(2,1)} %param.9) | copy-start | bytes 221188
  0.6 1.9 %copy-start.6 = (bf16[48,768]{1,0:T(8,128)(2,1)S(1)}, bf16[48,768]{1,0:T(8,128)(2,1)}, u32[]{:S(2)}) copy-start(bf16[48,768]{1,0:T(8,128)(2,1)} %param.10) | copy-start | bytes 221188
  2.2 50.1 %copy-start.8 = (bf16[768,16]{0,1:T(8,128)(2,1)S(1)}, bf16[768,16]{0,1:T(8,128)(2,1)}, u32[]{:S(2)}) copy-start(bf16[768,16]{0,1:T(8,128)(2,1)} %param.11) | copy-start | bytes 73732
  2.2 50.2 %copy-start = (bf16[2,256,768]{2,1,0:T(8,128)(2,1)S(1)}, bf16[2,256,768]{2,1,0:T(8,128)(2,1)}, u32[]{:S(2)}) copy-start(bf16[2,256,768]{2,1,0:T(8,128)(2,1)} %x_ref.3) | copy-start | bytes 2359300
  2.2 50.2 %copy-start.1 = (bf16[2,256,768]{2,1,0:T(8,128)(2,1)S(1)}, bf16[2,256,768]{2,1,0:T(8,128)(2,1)}, u32[]{:S(2)}) copy-start(bf16[2,256,768]{2,1,0:T(8,128)(2,1)} %g_ref.3) | copy-start | bytes 2359300
  52.5 1.1 copy-start.2
  53.6 1.1 copy-start.3
  54.7 14.4 %copy-start.9 = (f32[2]{0:T(128)S(1)}, f32[2]{0:T(128)}, u32[]{:S(2)}) copy-start(f32[2]{0:T(128)} %param.13) | copy-start | bytes 28
  113.7 37.1 %copy-start.4 = (bf16[32,32,640]{2,1,0:T(8,128)(2,1)S(1)}, bf16[32,32,640]{2,1,0:T(8,128)(2,1)}, u32[]{:S(2)}) copy-start(bf16[32,32,640]{2,1,0:T(8,128)(2,1)} %gather_features.1) | copy-start | bytes 3932164
  150.8 0.7 copy-start.5

commit v2 on v1

--- a/solution.py
+++ b/solution.py
@@ -88,7 +88,7 @@
             found.append((1, (z + step) % NZ))
         return found
 
-    for step in range(1, 11):
+    for step in range(1, 12):
         for way, zz in blocks_of(step):
             here = place(zz, y, low)
             wait_recv(here, z_recv.at[way, step])
@@ -97,7 +97,7 @@
                 start(remote(here, here, z_send.at[way, step + 1], z_recv.at[way, step + 1], target))
             send_y(here, zz)
             send_x(here, zz, y)
-        for way, zz in blocks_of(step - 1):
+        for way, zz in blocks_of(step - 2):
             below, above = place(zz, y_down, low), place(zz, y_up, low)
             wait_recv(below, y_recv.at[0, zz])
             wait_recv(above, y_recv.at[1, zz])
@@ -107,7 +107,7 @@
                 start(remote(above, above, o_send.at[zz], o_recv.at[zz], device(x, y_down, z, core)))
             send_x(below, zz, y_down)
             send_x(above, zz, y_up)
-        for way, zz in blocks_of(step - 2):
+        for way, zz in blocks_of(step - 3):
             far = (y + 2) % NY
             wait_recv(place(zz, far, low), o_recv.at[zz])
             send_x(place(zz, far, low), zz, far)
@@ -148,31 +148,31 @@
 
 def features_kernel(
     own_ref, other_ref, targets_ref, f_ref, got, zbuf, wide,
-    swap_send, swap_recv, a_send, a_recv, b_send, b_recv, y_send, y_recv, x_send, x_recv, c_send, c_recv,
+    swap_send, swap_recv, z_send, z_recv, y_send, y_recv, x_send, x_recv, c_send, c_recv,
 ):
     x, y, z, core = position()
-    high, low = z // 4, z % 4
-    near = [device(x, y, high * 4 + (low + d) % 4, core) for d in range(1, 4)]
-    far = [device(x, y, ((high + d) % 4) * 4 + low, core) for d in range(1, 4)]
+    along_z = [device(x, y, (z + d) % NZ, core) for d in range(1, NZ)]
     along_y = [device(x, (y + d) % NY, z, core) for d in range(1, 4)]
     along_x = [device((x + d) % NX, y, z, core) for d in range(1, 4)]
     partner = device(x, y, z, 1 - core)
-    greet(near + far + along_y + along_x + [partner])
+    greet(along_z + along_y + along_x + [partner])
 
     def remote(src, dst, send, recv, target):
         return pltpu.make_async_remote_copy(
             src_ref=src, dst_ref=dst, send_sem=send, recv_sem=recv, device_id=target, device_id_type=MESH
         )
 
-    def exchange(mine, theirs, send, recv, partners):
+    def begin(mine, send, recv, partners):
         copies = []
         for d, target in enumerate(partners):
             copy = remote(mine, mine, send.at[d], recv.at[d], target)
             copy.start()
             copies.append(copy)
-        for d in range(len(partners)):
-            remote(theirs[d], theirs[d], send.at[d], recv.at[d], partners[d]).wait_recv()
         return copies
+
+    def finish(theirs, send, recv, partners):
+        for d, target in enumerate(partners):
+            remote(theirs[d], theirs[d], send.at[d], recv.at[d], target).wait_recv()
 
     swap = remote(other_ref, got, swap_send, swap_recv, partner)
     swap.start()
@@ -188,29 +188,25 @@
     zbuf[z, :, 0:size] = feats.astype(jnp.bfloat16)
     zbuf[z, :, size:] = tail.astype(jnp.bfloat16)
     sends = [swap]
-    sends += exchange(
-        zbuf.at[z], [zbuf.at[high * 4 + (low + 4 - d) % 4] for d in range(1, 4)], a_send, a_recv, near
-    )
-    sends += exchange(
-        zbuf.at[pl.ds(high * 4, 4)],
-        [zbuf.at[pl.ds(((high + 4 - d) % 4) * 4, 4)] for d in range(1, 4)],
-        b_send, b_recv, far,
-    )
+    sends += begin(zbuf.at[z], z_send, z_recv, along_z)
+    finish([zbuf.at[(z + NZ - d) % NZ] for d in range(1, NZ)], z_send, z_recv, along_z)
     for zz in range(NZ):
         wide[2 * zz:2 * zz + 2, :] = zbuf[zz].astype(jnp.float32)
-    base = core * 16 + x * 4
-    f_ref[base + y] = wide[...].astype(jnp.bfloat16)
-    sends += exchange(
-        f_ref.at[base + y], [f_ref.at[base + (y + 4 - d) % NY] for d in range(1, 4)], y_send, y_recv, along_y
-    )
-    sends += exchange(
-        f_ref.at[pl.ds(base, 4)],
-        [f_ref.at[pl.ds(core * 16 + ((x + 4 - d) % NX) * 4, 4)] for d in range(1, 4)],
-        x_send, x_recv, along_x,
-    )
-    sends += exchange(
-        f_ref.at[pl.ds(core * 16, 16)], [f_ref.at[pl.ds((1 - core) * 16, 16)]], c_send, c_recv, [partner]
-    )
+    packed = wide[...].astype(jnp.bfloat16)
+    f_ref[core, x, y, 0] = packed[0:NZ]
+    f_ref[core, x, y, 1] = packed[NZ:]
+    ys = [(y + 4 - d) % NY for d in range(1, 4)]
+    xs = [(x + 4 - d) % NX for d in range(1, 4)]
+    sends += begin(f_ref.at[core, x, y, 0], y_send.at[0], y_recv.at[0], along_y)
+    sends += begin(f_ref.at[core, x, y, 1], x_send.at[0], x_recv.at[0], along_x)
+    finish([f_ref.at[core, x, yy, 0] for yy in ys], y_send.at[0], y_recv.at[0], along_y)
+    sends += begin(f_ref.at[core, x, :, 0], x_send.at[1], x_recv.at[1], along_x)
+    finish([f_ref.at[core, xx, y, 1] for xx in xs], x_send.at[0], x_recv.at[0], along_x)
+    sends += begin(f_ref.at[core, :, y, 1], y_send.at[1], y_recv.at[1], along_y)
+    finish([f_ref.at[core, xx, :, 0] for xx in xs], x_send.at[1], x_recv.at[1], along_x)
+    finish([f_ref.at[core, :, yy, 1] for yy in ys], y_send.at[1], y_recv.at[1], along_y)
+    sends += begin(f_ref.at[core], c_send, c_recv, [partner])
+    finish([f_ref.at[1 - core]], c_send, c_recv, [partner])
     for copy in sends:
         copy.wait_send()
 
@@ -221,40 +217,39 @@
     sem = pltpu.SemaphoreType.DMA
     return pl.pallas_call(
         features_kernel,
-        out_shape=jax.ShapeDtypeStruct((32, 32, size + 128), jnp.bfloat16),
+        out_shape=jax.ShapeDtypeStruct((2, NX, NY, 2, NZ, size + 128), jnp.bfloat16),
         in_specs=[inside] * 3,
         out_specs=inside,
         scratch_shapes=[
             pltpu.VMEM((2, size), jnp.float32),
             pltpu.VMEM((NZ, 2, size + 128), jnp.bfloat16),
             pltpu.VMEM((32, size + 128), jnp.float32),
-            sem, sem, sem((3,)), sem((3,)), sem((3,)), sem((3,)), sem((3,)), sem((3,)),
-            sem((3,)), sem((3,)), sem((1,)), sem((1,)),
+            sem, sem, sem((NZ - 1,)), sem((NZ - 1,)), sem((2, 3)), sem((2, 3)), sem((2, 3)), sem((2, 3)),
+            sem((1,)), sem((1,)),
         ],
         compiler_params=pltpu.CompilerParams(collective_id=1, has_side_effects=True),
         name="gather_features",
     )(own, other, targets)
 
 
-def invert(m):
+def invert(m, width=8):
     side = m.shape[0]
     lane = lax.broadcasted_iota(jnp.int32, m.shape, 1)
     sub = lax.broadcasted_iota(jnp.int32, m.shape, 0)
-    for k in range(0, side, 2):
-        j = k + 1
-        c0 = jnp.broadcast_to(m[:, k:k + 1], m.shape)
-        c1 = jnp.broadcast_to(m[:, j:j + 1], m.shape)
-        inv0 = 1.0 / c0[k:k + 1, :]
-        r0 = jnp.where(lane[0:1] == k, 1.0, m[k:k + 1, :]) * inv0
-        r1 = jnp.where(lane[0:1] == k, 0.0, m[j:j + 1, :]) - c0[j:j + 1, :] * r0
-        across = c1[k:k + 1, :] * inv0
-        inv1 = 1.0 / (c1[j:j + 1, :] - c0[j:j + 1, :] * across)
-        r1 = jnp.where(lane[0:1] == j, 1.0, r1) * inv1
-        c0 = jnp.where(sub == k, -1.0, c0)
-        c1 = jnp.where(sub == k, 0.0, c1) - c0 * across
-        c1 = jnp.where(sub == j, -1.0, c1)
-        m = jnp.where((lane == k) | (sub == k), 0.0, m) - c0 * r0
-        m = jnp.where((lane == j) | (sub == j), 0.0, m) - c1 * r1
+    for k in range(0, side, width):
+        columns = [jnp.broadcast_to(m[:, k + i:k + i + 1], m.shape) for i in range(width)]
+        rows = [m[k + i:k + i + 1, :] for i in range(width)]
+        for i in range(width):
+            at = k + i
+            column = columns[i]
+            inverse = 1.0 / column[at:at + 1, :]
+            row = jnp.where(lane[0:1] == at, 1.0, rows[i]) * inverse
+            swept = jnp.where(sub == at, -1.0, column)
+            for j in range(i + 1, width):
+                to = k + j
+                rows[j] = jnp.where(lane[0:1] == at, 0.0, rows[j]) - column[to:to + 1, :] * row
+                columns[j] = jnp.where(sub == at, 0.0, columns[j]) - swept * (columns[j][at:at + 1, :] * inverse)
+            m = jnp.where((lane == at) | (sub == at), 0.0, m) - swept * row
     return m
 
 

time: 153 us -> 139 us (0.908)
  Pallas kernels: 139 us -> 125 us
    pallas_call x1, Pallas kernels: 37 us -> 27.8 us  [solve(): pl.pallas_call(solve_kernel, out_shape=jax.ShapeDtypeStruct((8, extended....]
    pallas_call x1, Pallas kernels: 40.2 us -> 33.7 us  [gather_features(): pl.pallas_call(features_kernel, out_shape=jax.ShapeDtypeStruct((2, NX, NY...]
    pallas_call x1, Pallas kernels: 49.1 us -> 50.7 us  [gather_weights(): pl.pallas_call(weights_kernel, out_shape=(jax.ShapeDtypeStruct((2, NZ, 2,...]
where the time goes in v2:
time: 139 us
  Pallas kernels  125 us (90%)
  local copies, waits for them, and re-layouts  7.45 us (5%)
  matrix products  4.36 us (3%)
    pallas_call x1, Pallas kernels, gather_weights(): pl.pallas_call(weights_kernel, out_shape=(jax.ShapeDtypeStruct((2, NZ, 2,...  50.7 us
    pallas_call x1, Pallas kernels, gather_features(): pl.pallas_call(features_kernel, out_shape=jax.ShapeDtypeStruct((2, NX, NY...  33.7 us
    pallas_call x1, Pallas kernels, solve(): pl.pallas_call(solve_kernel, out_shape=jax.ShapeDtypeStruct((8, extended....  27.8 us
    pallas_call x1, Pallas kernels, partial_features(): pl.pallas_call(block_kernel, grid=(hidden_units // chunk,), out_shape=jax...  13 us
    dot_general x1, matrix products, per_device(): lax.dot_general(everyone, table, (((0,), (0,)), ((), ())), preferred_elem...  3.71 us
    unnamed x22, local copies, waits for them, and re-layouts  3.28 us

profile of v2, /device:TPU:1, one launch (start us, length us, event | category | flops | bytes accessed | tf_op | source)
XLA Modules:
  0.0 138.5 jit_solution(215939638422888808)
XLA Ops:
  0.6 0.0 copy-start.7
  0.6 0.0 copy-start.6
  0.7 1.2 reshape.29
  1.9 0.3 constant_dynamic-slice_fusion
  2.2 0.0 copy-start.8
  2.2 0.0 copy-start
  2.2 0.0 copy-start.1
  2.2 0.3 copy.12
  2.5 0.0 copy-done.7
  2.5 0.0 copy-done.6
  2.5 0.7 pad_maximum_fusion.w_ref
  3.2 50.7 %gather_weights.1 = (bf16[2,16,2,2,24,768]{5,4,3,2,1,0:T(8,128)(2,1)}, bf16[2,256,768]{2,1,0:T(8,128)(2,1)}, bf16[2,256,768]{2,1,0:T(8,128)(2,1)}) custom-call(bf16[2,256,768]{2,1,0:T(8,128)(2,1)} %x_ref.3, bf16[2,256,768]{2,1,0:T(8,128)(2,1)} %g_ref.3, bf16[2,2,24,768]{3,2,1,0:T(8,128)(2,1)} %pad_maximum_fusion.w_ref), custom_call_target="tpu_custom_call" | custom-call | tf_op jit(solution)/shard_map/gather_weights/pallas_call | solution.py:131
  53.9 0.0 copy-done.8
  53.9 0.2 copy.10.sketch_in_ref
  54.1 0.0 copy-done
  54.1 0.0 copy-done.1
  54.1 0.0 copy-start.2
  54.1 1.1 copy-done.2
  55.2 0.0 copy-start.3
  55.2 1.1 copy-done.3
  56.3 0.0 copy-start.9
  56.3 13.0 %pointwise_block.1 = f32[4,2,16,16]{3,2,1,0:T(8,128)S(1)} custom-call(bf16[2,256,768]{2,1,0:T(8,128)(2,1)S(1)} %copy-done, bf16[2,256,768]{2,1,0:T(8,128)(2,1)S(1)} %copy-done.1, bf16[2,256,768]{2,1,0:T(8,128)(2,1)S(1)} %copy-done.2, bf16[2,256,768]{2,1,0:T(8,128)(2,1)S(1)} %copy-done.3, bf16[2,1536,768]{2,1,0:T(8,128)(2,1)} %bitcast.24, ...), custom_call_target="tpu_custom_call" | custom-call | tf_op jit(solution)/shard_map/pointwise_block/pallas_call | solution.py:331
  69.4 0.7 slice.19.own_ref
  70.1 0.7 slice.21.other_ref
  70.7 0.0 copy-done.9
  70.7 0.6 copy.11.targets_ref
  71.4 33.7 %gather_features.1 = bf16[2,4,4,2,16,640]{5,4,3,2,1,0:T(8,128)(2,1)} custom-call(f32[2,512]{1,0:T(2,128)} %slice.19.own_ref, f32[2,512]{1,0:T(2,128)} %slice.21.other_ref, f32[2,1]{1,0:T(2,128)} %copy.11.targets_ref), custom_call_target="tpu_custom_call" | custom-call | tf_op jit(solution)/shard_map/gather_features/pallas_call | solution.py:218
  105.1 3.7 %fusion.6.a_ref = f32[512,640]{1,0:T(8,128)} fusion(bf16[1024,640]{1,0:T(8,128)(2,1)} %bitcast.25), kind=kOutput, calls=%fused_computation.9 | convolution fusion | flops 671088640 | bytes 3670016 | tf_op jit(solution)/shard_map/dot_general | solution.py:366
  108.8 0.0 copy-start.4
  108.8 27.8 %solve.1 = f32[8,512]{1,0:T(8,128)} custom-call(f32[512,640]{1,0:T(8,128)} %fusion.6.a_ref), custom_call_target="tpu_custom_call" | custom-call | tf_op jit(solution)/shard_map/solve/pallas_call | solution.py:281
  136.6 0.0 copy-done.4
  136.6 0.0 copy-start.5
  136.6 0.1 slice.26
  136.7 0.6 copy-done.5
  137.3 0.6 fusion.1
  138.0 0.6 slice.27
  (1 shorter events, 0.0 us)
Async XLA Ops:
  0.6 1.9 %copy-start.7 = (bf16[48,768]{1,0:T(8,128)(2,1)S(1)}, bf16[48,768]{1,0:T(8,128)(2,1)}, u32[]{:S(2)}) copy-start(bf16[48,768]{1,0:T(8,128)(2,1)} %param.9) | copy-start | bytes 221188
  0.6 1.9 %copy-start.6 = (bf16[48,768]{1,0:T(8,128)(2,1)S(1)}, bf16[48,768]{1,0:T(8,128)(2,1)}, u32[]{:S(2)}) copy-start(bf16[48,768]{1,0:T(8,128)(2,1)} %param.10) | copy-start | bytes 221188
  2.2 51.7 %copy-start.8 = (bf16[768,16]{0,1:T(8,128)(2,1)S(1)}, bf16[768,16]{0,1:T(8,128)(2,1)}, u32[]{:S(2)}) copy-start(bf16[768,16]{0,1:T(8,128)(2,1)} %param.11) | copy-start | bytes 73732
  2.2 51.8 %copy-start = (bf16[2,256,768]{2,1,0:T(8,128)(2,1)S(1)}, bf16[2,256,768]{2,1,0:T(8,128)(2,1)}, u32[]{:S(2)}) copy-start(bf16[2,256,768]{2,1,0:T(8,128)(2,1)} %x_ref.3) | copy-start | bytes 2359300
  2.2 51.8 %copy-start.1 = (bf16[2,256,768]{2,1,0:T(8,128)(2,1)S(1)}, bf16[2,256,768]{2,1,0:T(8,128)(2,1)}, u32[]{:S(2)}) copy-start(bf16[2,256,768]{2,1,0:T(8,128)(2,1)} %g_ref.3) | copy-start | bytes 2359300
  54.1 1.1 copy-start.2
  55.2 1.1 copy-start.3
  56.3 14.4 %copy-start.9 = (f32[2]{0:T(128)S(1)}, f32[2]{0:T(128)}, u32[]{:S(2)}) copy-start(f32[2]{0:T(128)} %param.13) | copy-start | bytes 28
  108.8 27.8 %copy-start.4 = (bf16[2,4,4,2,16,640]{5,4,3,2,1,0:T(8,128)(2,1)S(1)}, bf16[2,4,4,2,16,640]{5,4,3,2,1,0:T(8,128)(2,1)}, u32[]{:S(2)}) copy-start(bf16[2,4,4,2,16,640]{5,4,3,2,1,0:T(8,128)(2,1)} %gather_features.1) | copy-start | bytes 3932164
  136.6 0.7 copy-start.5

commit v3 on v2

--- a/solution.py
+++ b/solution.py
@@ -34,10 +34,12 @@
     x, y, z, core = position()
     low = x % 2
     up, down = (z + 1) % NZ, (z + NZ - 1) % NZ
+    up2, down2 = (z + 2) % NZ, (z + NZ - 2) % NZ
     y_up, y_down = (y + 1) % NY, (y + NY - 1) % NY
     x_up, x_down = (x + 1) % NX, (x + NX - 1) % NX
     greet([
         device(x, y, up, core), device(x, y, down, core),
+        device(x, y, up2, core), device(x, y, down2, core),
         device(x, y_up, z, core), device(x, y_down, z, core),
         device(x_up, y, z, core), device(x_down, y, z, core),
         device(x, y, z, 1 - core),
@@ -70,6 +72,8 @@
     mine = w_ref.at[y // 2, y % 2]
     start(remote(mine, place(z, y, low), z_send.at[0, 1], z_recv.at[0, 1], device(x, y, up, core)))
     start(remote(mine, place(z, y, low), z_send.at[1, 1], z_recv.at[1, 1], device(x, y, down, core)))
+    start(remote(mine, place(z, y, low), z_send.at[0, 2], z_recv.at[0, 2], device(x, y, up2, core)))
+    start(remote(mine, place(z, y, low), z_send.at[1, 2], z_recv.at[1, 2], device(x, y, down2, core)))
     for q in range(4):
         send_x(w_ref.at[q // 2, q % 2], z, q)
     locals_ = []
@@ -92,9 +96,9 @@
         for way, zz in blocks_of(step):
             here = place(zz, y, low)
             wait_recv(here, z_recv.at[way, step])
-            if step < (8 if way == 0 else 7):
-                target = device(x, y, up if way == 0 else down, core)
-                start(remote(here, here, z_send.at[way, step + 1], z_recv.at[way, step + 1], target))
+            if step + 2 <= (8 if way == 0 else 7):
+                target = device(x, y, up2 if way == 0 else down2, core)
+                start(remote(here, here, z_send.at[way, step + 2], z_recv.at[way, step + 2], target))
             send_y(here, zz)
             send_x(here, zz, y)
         for way, zz in blocks_of(step - 2):

time: 139 us -> 133 us (0.957)
  Pallas kernels: 125 us -> 119 us
    pallas_call x1, Pallas kernels: 33.7 us -> 30.4 us  [gather_features(): pl.pallas_call(features_kernel, out_shape=jax.ShapeDtypeStruct((2, NX, NY...]
    pallas_call x1, Pallas kernels: 50.7 us -> 48.1 us  [gather_weights(): pl.pallas_call(weights_kernel, out_shape=(jax.ShapeDtypeStruct((2, NZ, 2,...]
where the time goes in v3:
time: 133 us
  Pallas kernels  119 us (89%)
  local copies, waits for them, and re-layouts  7.45 us (6%)
  matrix products  4.36 us (3%)
    pallas_call x1, Pallas kernels, gather_weights(): pl.pallas_call(weights_kernel, out_shape=(jax.ShapeDtypeStruct((2, NZ, 2,...  48.1 us
    pallas_call x1, Pallas kernels, gather_features(): pl.pallas_call(features_kernel, out_shape=jax.ShapeDtypeStruct((2, NX, NY...  30.4 us
    pallas_call x1, Pallas kernels, solve(): pl.pallas_call(solve_kernel, out_shape=jax.ShapeDtypeStruct((8, extended....  27.8 us
    pallas_call x1, Pallas kernels, partial_features(): pl.pallas_call(block_kernel, grid=(hidden_units // chunk,), out_shape=jax...  13 us
    dot_general x1, matrix products, per_device(): lax.dot_general(everyone, table, (((0,), (0,)), ((), ())), preferred_elem...  3.71 us
    unnamed x22, local copies, waits for them, and re-layouts  3.28 us

profile of v3, /device:TPU:1, one launch (start us, length us, event | category | flops | bytes accessed | tf_op | source)
XLA Modules:
  0.0 132.7 jit_solution(12575775763737045351)
XLA Ops:
  0.6 0.0 copy-start.7
  0.6 0.0 copy-start.6
  0.7 1.2 reshape.29
  1.9 0.3 constant_dynamic-slice_fusion
  2.2 0.0 copy-start.8
  2.2 0.0 copy-start
  2.2 0.0 copy-start.1
  2.2 0.3 copy.12
  2.5 0.0 copy-done.7
  2.5 0.0 copy-done.6
  2.5 0.7 pad_maximum_fusion.w_ref
  3.2 48.1 %gather_weights.1 = (bf16[2,16,2,2,24,768]{5,4,3,2,1,0:T(8,128)(2,1)}, bf16[2,256,768]{2,1,0:T(8,128)(2,1)}, bf16[2,256,768]{2,1,0:T(8,128)(2,1)}) custom-call(bf16[2,256,768]{2,1,0:T(8,128)(2,1)} %x_ref.3, bf16[2,256,768]{2,1,0:T(8,128)(2,1)} %g_ref.3, bf16[2,2,24,768]{3,2,1,0:T(8,128)(2,1)} %pad_maximum_fusion.w_ref), custom_call_target="tpu_custom_call" | custom-call | tf_op jit(solution)/shard_map/gather_weights/pallas_call | solution.py:135
  51.3 0.0 copy-done.8
  51.3 0.2 copy.10.sketch_in_ref
  51.5 0.0 copy-done
  51.5 0.0 copy-done.1
  51.5 0.0 copy-start.2
  51.5 1.1 copy-done.2
  52.6 0.0 copy-start.3
  52.6 1.1 copy-done.3
  53.7 0.0 copy-start.9
  53.7 13.0 %pointwise_block.1 = f32[4,2,16,16]{3,2,1,0:T(8,128)S(1)} custom-call(bf16[2,256,768]{2,1,0:T(8,128)(2,1)S(1)} %copy-done, bf16[2,256,768]{2,1,0:T(8,128)(2,1)S(1)} %copy-done.1, bf16[2,256,768]{2,1,0:T(8,128)(2,1)S(1)} %copy-done.2, bf16[2,256,768]{2,1,0:T(8,128)(2,1)S(1)} %copy-done.3, bf16[2,1536,768]{2,1,0:T(8,128)(2,1)} %bitcast.24, ...), custom_call_target="tpu_custom_call" | custom-call | tf_op jit(solution)/shard_map/pointwise_block/pallas_call | solution.py:335
  66.8 0.7 slice.19.own_ref
  67.5 0.7 slice.21.other_ref
  68.1 0.0 copy-done.9
  68.1 0.6 copy.11.targets_ref
  68.8 30.4 %gather_features.1 = bf16[2,4,4,2,16,640]{5,4,3,2,1,0:T(8,128)(2,1)} custom-call(f32[2,512]{1,0:T(2,128)} %slice.19.own_ref, f32[2,512]{1,0:T(2,128)} %slice.21.other_ref, f32[2,1]{1,0:T(2,128)} %copy.11.targets_ref), custom_call_target="tpu_custom_call" | custom-call | tf_op jit(solution)/shard_map/gather_features/pallas_call | solution.py:222
  99.2 3.7 %fusion.6.a_ref = f32[512,640]{1,0:T(8,128)} fusion(bf16[1024,640]{1,0:T(8,128)(2,1)} %bitcast.25), kind=kOutput, calls=%fused_computation.9 | convolution fusion | flops 671088640 | bytes 3670016 | tf_op jit(solution)/shard_map/dot_general | solution.py:370
  102.9 0.0 copy-start.4
  102.9 27.8 %solve.1 = f32[8,512]{1,0:T(8,128)} custom-call(f32[512,640]{1,0:T(8,128)} %fusion.6.a_ref), custom_call_target="tpu_custom_call" | custom-call | tf_op jit(solution)/shard_map/solve/pallas_call | solution.py:285
  130.7 0.0 copy-done.4
  130.7 0.0 copy-start.5
  130.7 0.1 slice.26
  130.9 0.6 copy-done.5
  131.4 0.6 fusion.1
  132.1 0.6 slice.27
  (1 shorter events, 0.0 us)
Async XLA Ops:
  0.6 1.9 %copy-start.7 = (bf16[48,768]{1,0:T(8,128)(2,1)S(1)}, bf16[48,768]{1,0:T(8,128)(2,1)}, u32[]{:S(2)}) copy-start(bf16[48,768]{1,0:T(8,128)(2,1)} %param.9) | copy-start | bytes 221188
  0.6 1.9 %copy-start.6 = (bf16[48,768]{1,0:T(8,128)(2,1)S(1)}, bf16[48,768]{1,0:T(8,128)(2,1)}, u32[]{:S(2)}) copy-start(bf16[48,768]{1,0:T(8,128)(2,1)} %param.10) | copy-start | bytes 221188
  2.2 49.1 %copy-start.8 = (bf16[768,16]{0,1:T(8,128)(2,1)S(1)}, bf16[768,16]{0,1:T(8,128)(2,1)}, u32[]{:S(2)}) copy-start(bf16[768,16]{0,1:T(8,128)(2,1)} %param.11) | copy-start | bytes 73732
  2.2 49.2 %copy-start = (bf16[2,256,768]{2,1,0:T(8,128)(2,1)S(1)}, bf16[2,256,768]{2,1,0:T(8,128)(2,1)}, u32[]{:S(2)}) copy-start(bf16[2,256,768]{2,1,0:T(8,128)(2,1)} %x_ref.3) | copy-start | bytes 2359300
  2.2 49.2 %copy-start.1 = (bf16[2,256,768]{2,1,0:T(8,128)(2,1)S(1)}, bf16[2,256,768]{2,1,0:T(8,128)(2,1)}, u32[]{:S(2)}) copy-start(bf16[2,256,768]{2,1,0:T(8,128)(2,1)} %g_ref.3) | copy-start | bytes 2359300
  51.5 1.1 copy-start.2
  52.6 1.1 copy-start.3
  53.7 14.4 %copy-start.9 = (f32[2]{0:T(128)S(1)}, f32[2]{0:T(128)}, u32[]{:S(2)}) copy-start(f32[2]{0:T(128)} %param.13) | copy-start | bytes 28
  102.9 27.8 %copy-start.4 = (bf16[2,4,4,2,16,640]{5,4,3,2,1,0:T(8,128)(2,1)S(1)}, bf16[2,4,4,2,16,640]{5,4,3,2,1,0:T(8,128)(2,1)}, u32[]{:S(2)}) copy-start(bf16[2,4,4,2,16,640]{5,4,3,2,1,0:T(8,128)(2,1)} %gather_features.1) | copy-start | bytes 3932164
  130.7 0.7 copy-start.5

commit v4 on v3

--- a/solution.py
+++ b/solution.py
@@ -92,7 +92,7 @@
             found.append((1, (z + step) % NZ))
         return found
 
-    for step in range(1, 12):
+    for step in range(1, 11):
         for way, zz in blocks_of(step):
             here = place(zz, y, low)
             wait_recv(here, z_recv.at[way, step])
@@ -101,7 +101,7 @@
                 start(remote(here, here, z_send.at[way, step + 2], z_recv.at[way, step + 2], target))
             send_y(here, zz)
             send_x(here, zz, y)
-        for way, zz in blocks_of(step - 2):
+        for way, zz in blocks_of(step - 1):
             below, above = place(zz, y_down, low), place(zz, y_up, low)
             wait_recv(below, y_recv.at[0, zz])
             wait_recv(above, y_recv.at[1, zz])
@@ -111,7 +111,7 @@
                 start(remote(above, above, o_send.at[zz], o_recv.at[zz], device(x, y_down, z, core)))
             send_x(below, zz, y_down)
             send_x(above, zz, y_up)
-        for way, zz in blocks_of(step - 3):
+        for way, zz in blocks_of(step - 2):
             far = (y + 2) % NY
             wait_recv(place(zz, far, low), o_recv.at[zz])
             send_x(place(zz, far, low), zz, far)

time: 133 us -> 133 us (level)
  no operation moved by 1% of the time
where the time goes in v4:
time: 133 us; the launch traced here: 132 us
  Pallas kernels  119 us (89%)
  local copies, waits for them, and re-layouts  7.45 us (6%)
  matrix products  4.36 us (3%)
    pallas_call x1, Pallas kernels, gather_weights(): pl.pallas_call(weights_kernel, out_shape=(jax.ShapeDtypeStruct((2, NZ, 2,...  48.3 us
    pallas_call x1, Pallas kernels, gather_features(): pl.pallas_call(features_kernel, out_shape=jax.ShapeDtypeStruct((2, NX, NY...  29.8 us
    pallas_call x1, Pallas kernels, solve(): pl.pallas_call(solve_kernel, out_shape=jax.ShapeDtypeStruct((8, extended....  27.8 us
    pallas_call x1, Pallas kernels, partial_features(): pl.pallas_call(block_kernel, grid=(hidden_units // chunk,), out_shape=jax...  13 us
    dot_general x1, matrix products, per_device(): lax.dot_general(everyone, table, (((0,), (0,)), ((), ())), preferred_elem...  3.71 us
    unnamed x22, local copies, waits for them, and re-layouts  3.28 us

profile of v4, /device:TPU:1, one launch (start us, length us, event | category | flops | bytes accessed | tf_op | source)
XLA Modules:
  0.0 132.3 jit_solution(10390788970421739910)
XLA Ops:
  0.6 0.0 copy-start.7
  0.6 0.0 copy-start.6
  0.7 1.2 reshape.29
  1.9 0.3 constant_dynamic-slice_fusion
  2.2 0.0 copy-start.8
  2.2 0.0 copy-start
  2.2 0.0 copy-start.1
  2.2 0.3 copy.12
  2.5 0.0 copy-done.7
  2.5 0.0 copy-done.6
  2.5 0.7 pad_maximum_fusion.w_ref
  3.2 48.3 %gather_weights.1 = (bf16[2,16,2,2,24,768]{5,4,3,2,1,0:T(8,128)(2,1)}, bf16[2,256,768]{2,1,0:T(8,128)(2,1)}, bf16[2,256,768]{2,1,0:T(8,128)(2,1)}) custom-call(bf16[2,256,768]{2,1,0:T(8,128)(2,1)} %x_ref.3, bf16[2,256,768]{2,1,0:T(8,128)(2,1)} %g_ref.3, bf16[2,2,24,768]{3,2,1,0:T(8,128)(2,1)} %pad_maximum_fusion.w_ref), custom_call_target="tpu_custom_call" | custom-call | tf_op jit(solution)/shard_map/gather_weights/pallas_call | solution.py:135
  51.5 0.0 copy-done.8
  51.5 0.2 copy.10.sketch_in_ref
  51.7 0.0 copy-done
  51.7 0.0 copy-done.1
  51.7 0.0 copy-start.2
  51.7 1.1 copy-done.2
  52.8 0.0 copy-start.3
  52.8 1.1 copy-done.3
  54.0 0.0 copy-start.9
  54.0 13.0 %pointwise_block.1 = f32[4,2,16,16]{3,2,1,0:T(8,128)S(1)} custom-call(bf16[2,256,768]{2,1,0:T(8,128)(2,1)S(1)} %copy-done, bf16[2,256,768]{2,1,0:T(8,128)(2,1)S(1)} %copy-done.1, bf16[2,256,768]{2,1,0:T(8,128)(2,1)S(1)} %copy-done.2, bf16[2,256,768]{2,1,0:T(8,128)(2,1)S(1)} %copy-done.3, bf16[2,1536,768]{2,1,0:T(8,128)(2,1)} %bitcast.24, ...), custom_call_target="tpu_custom_call" | custom-call | tf_op jit(solution)/shard_map/pointwise_block/pallas_call | solution.py:335
  67.0 0.7 slice.19.own_ref
  67.7 0.7 slice.21.other_ref
  68.4 0.0 copy-done.9
  68.4 0.6 copy.11.targets_ref
  69.0 29.8 %gather_features.1 = bf16[2,4,4,2,16,640]{5,4,3,2,1,0:T(8,128)(2,1)} custom-call(f32[2,512]{1,0:T(2,128)} %slice.19.own_ref, f32[2,512]{1,0:T(2,128)} %slice.21.other_ref, f32[2,1]{1,0:T(2,128)} %copy.11.targets_ref), custom_call_target="tpu_custom_call" | custom-call | tf_op jit(solution)/shard_map/gather_features/pallas_call | solution.py:222
  98.8 3.7 %fusion.6.a_ref = f32[512,640]{1,0:T(8,128)} fusion(bf16[1024,640]{1,0:T(8,128)(2,1)} %bitcast.25), kind=kOutput, calls=%fused_computation.9 | convolution fusion | flops 671088640 | bytes 3670016 | tf_op jit(solution)/shard_map/dot_general | solution.py:370
  102.5 0.0 copy-start.4
  102.5 27.8 %solve.1 = f32[8,512]{1,0:T(8,128)} custom-call(f32[512,640]{1,0:T(8,128)} %fusion.6.a_ref), custom_call_target="tpu_custom_call" | custom-call | tf_op jit(solution)/shard_map/solve/pallas_call | solution.py:285
  130.3 0.0 copy-done.4
  130.3 0.0 copy-start.5
  130.3 0.1 slice.26
  130.5 0.6 copy-done.5
  131.0 0.6 fusion.1
  131.7 0.6 slice.27
  (1 shorter events, 0.0 us)
Async XLA Ops:
  0.6 1.9 %copy-start.7 = (bf16[48,768]{1,0:T(8,128)(2,1)S(1)}, bf16[48,768]{1,0:T(8,128)(2,1)}, u32[]{:S(2)}) copy-start(bf16[48,768]{1,0:T(8,128)(2,1)} %param.9) | copy-start | bytes 221188
  0.6 1.9 %copy-start.6 = (bf16[48,768]{1,0:T(8,128)(2,1)S(1)}, bf16[48,768]{1,0:T(8,128)(2,1)}, u32[]{:S(2)}) copy-start(bf16[48,768]{1,0:T(8,128)(2,1)} %param.10) | copy-start | bytes 221188
  2.2 49.3 %copy-start.8 = (bf16[768,16]{0,1:T(8,128)(2,1)S(1)}, bf16[768,16]{0,1:T(8,128)(2,1)}, u32[]{:S(2)}) copy-start(bf16[768,16]{0,1:T(8,128)(2,1)} %param.11) | copy-start | bytes 73732
  2.2 49.5 %copy-start = (bf16[2,256,768]{2,1,0:T(8,128)(2,1)S(1)}, bf16[2,256,768]{2,1,0:T(8,128)(2,1)}, u32[]{:S(2)}) copy-start(bf16[2,256,768]{2,1,0:T(8,128)(2,1)} %x_ref.3) | copy-start | bytes 2359300
  2.2 49.5 %copy-start.1 = (bf16[2,256,768]{2,1,0:T(8,128)(2,1)S(1)}, bf16[2,256,768]{2,1,0:T(8,128)(2,1)}, u32[]{:S(2)}) copy-start(bf16[2,256,768]{2,1,0:T(8,128)(2,1)} %g_ref.3) | copy-start | bytes 2359300
  51.7 1.1 copy-start.2
  52.8 1.1 copy-start.3
  54.0 14.4 %copy-start.9 = (f32[2]{0:T(128)S(1)}, f32[2]{0:T(128)}, u32[]{:S(2)}) copy-start(f32[2]{0:T(128)} %param.13) | copy-start | bytes 28
  102.5 27.8 %copy-start.4 = (bf16[2,4,4,2,16,640]{5,4,3,2,1,0:T(8,128)(2,1)S(1)}, bf16[2,4,4,2,16,640]{5,4,3,2,1,0:T(8,128)(2,1)}, u32[]{:S(2)}) copy-start(bf16[2,4,4,2,16,640]{5,4,3,2,1,0:T(8,128)(2,1)} %gather_features.1) | copy-start | bytes 3932164
  130.3 0.7 copy-start.5
